TPU v7x, 32 devices: a whole 2x2x4 slice. The times are simulated.
32 devices in a mesh: section: 2 (over core), tensor: 4 (over y, x), expert: 4 (over z).
Axes of the slice: x: 2, y: 2, z: 4, core: 2. Of those that a mesh axis runs over, the one named last changes fastest.
Arguments:
- tokens: bfloat16 [2, 4, 256, 768], P(None, 'expert', 'tensor'), may hold values from -6 to 6
- cotangent: float32 [2, 4, 256, 768], P(None, 'expert', 'tensor'), may hold values from -6 to 6
- norm_gains: float32 [2, 2, 768], P('section'), may hold values from 0.5 to 1.5
- norm_shifts: float32 [2, 2, 768], P('section'), may hold values from -3 to 3
- w_qkv: bfloat16 [2, 3, 768, 12, 64], P('section', None, None, 'tensor'), may hold values from -0.21875 to 0.21875
- w_attn_out: bfloat16 [2, 12, 64, 768], P('section', 'tensor'), may hold values from -0.21875 to 0.21875
- w_router: bfloat16 [2, 768, 8], P('section'), may hold values from -0.21875 to 0.21875
- w_in: bfloat16 [2, 8, 768, 3072], P('section', 'expert', None, 'tensor'), may hold values from -0.21875 to 0.21875
- w_out: bfloat16 [2, 8, 3072, 768], P('section', 'expert', 'tensor'), may hold values from -0.3125 to 0.3125
- choices: int32 [2, 2, 4, 256, 2], P('section', None, 'expert'), may hold values from 0 to 7, as said below
- slot_ranks: int32 [2, 2, 4, 256, 2], P('section', None, 'expert'), may hold values from 0 to 64, as said below
Outputs:
- section_out: bfloat16 [2, 2, 4, 256, 768], P('section', None, 'expert', 'tensor')
- input_grad: bfloat16 [2, 2, 4, 256, 768], P('section', None, 'expert', 'tensor')
- grad_norm_gains: float32 [2, 2, 768], P('section')
- grad_norm_shifts: float32 [2, 2, 768], P('section')
- grad_w_qkv: float32 [2, 3, 768, 12, 64], P('section', None, None, 'tensor')
- grad_w_attn_out: float32 [2, 12, 64, 768], P('section', 'tensor')
- grad_w_router: float32 [2, 768, 8], P('section')
- grad_w_in: float32 [2, 8, 768, 3072], P('section', 'expert', None, 'tensor')
- grad_w_out: float32 [2, 8, 3072, 768], P('section', 'expert', 'tensor')
Inputs may be any that keep to these rules, and one draw needn't show every extreme that they name: `choices`: the two experts of a token differ. slot_ranks[s, m, row, k] counts the earlier entries that name the same expert in the same block of 256 rows (one index of the expert axis, one section, one micro-batch), where all first choices of the block come before all second choices and rows go in order; it is 64 where that count is 64 or more.
All inputs are finite; a program needn't handle non-finite values.
Results may differ from a plain program's by a relative error of at most 0.025.
Values may be sent and summed in bfloat16 or wider, within the bound.
No kernel may reach another device: no remote copies, remote signals or barrier semaphores. Data moves between devices by JAX's collectives and lax.ppermute only.
A program may use at most 128 MiB of HBM per device.

v0:
```python
import jax
import jax.numpy as jnp
from jax import lax
from jax.sharding import PartitionSpec as P

HEAD_DIM = 64
norm_eps = 1e-06
half_root = 0.7071067811865476
tau_root = 0.3989422804014327
highest = lax.Precision.HIGHEST


def shifted(block, axis, distance):
    devices = range(lax.axis_size(axis))
    route = [(i - distance, i) for i in devices if i - distance in devices]
    return lax.ppermute(block, axis, route)


def gelu_value(values):
    return 0.5 * values * (1.0 + lax.erf(values * half_root))


def gelu_slope(values):
    return (
        0.5 * (1.0 + lax.erf(values * half_root))
        + values * jnp.exp(-0.5 * values * values) * tau_root
    )


def normalize(values, gain_row, shift_row):
    center = jnp.mean(values, axis=-1, keepdims=True)
    deviation = values - center
    factor = lax.rsqrt(jnp.mean(deviation * deviation, axis=-1, keepdims=True) + norm_eps)
    unit_rows = deviation * factor
    return (unit_rows * gain_row + shift_row, unit_rows, factor)


def norm_back(grad_norm, unit_rows, factor, gain_row):
    scaled = grad_norm * gain_row
    return factor * (
        scaled
        - jnp.mean(scaled, axis=-1, keepdims=True)
        - unit_rows * jnp.mean(scaled * unit_rows, axis=-1, keepdims=True)
    )


def gather_rows(block_part):
    return lax.all_gather(block_part, "tensor", axis=1, tiled=True)


def sum_rows(block_terms):
    return lax.psum_scatter(
        block_terms.astype(jnp.bfloat16), "tensor", scatter_dimension=1, tiled=True
    ).astype(jnp.float32)


def forward(block_rows, weights_all, expert_picks, slot_picks):
    gain_rows, shift_rows, w_qkv, w_attn, w_router, w_first, w_second = weights_all
    images = expert_picks.shape[0]
    length = expert_picks.shape[1]
    feature_count = block_rows.shape[2]
    experts = w_router.shape[1]
    capacity = 2 * images * length // experts
    dump_cell = experts * capacity
    owner_count = lax.axis_size("expert")
    local_count = experts // owner_count
    score_scale = HEAD_DIM ** (-0.5)
    head_count = w_qkv.shape[2] // HEAD_DIM
    start_rows = block_rows.astype(jnp.float32)
    normed_one, unit_one, factor_one = normalize(start_rows, gain_rows[0], shift_rows[0])
    full_one = gather_rows(normed_one.astype(jnp.bfloat16))
    qkv_rows = jnp.einsum(
        "isd,kdh->kish", full_one, w_qkv, preferred_element_type=jnp.float32
    ).astype(jnp.bfloat16)
    qkv_heads = qkv_rows.reshape(3, images, length, head_count, HEAD_DIM)
    scores = (
        jnp.einsum(
            "ishd,ithd->ihst", qkv_heads[0], qkv_heads[1], preferred_element_type=jnp.float32
        )
        * score_scale
    )
    log_total = jnp.log(jnp.sum(jnp.exp(scores), axis=-1, keepdims=True))
    weights_soft = jnp.exp(scores - log_total).astype(jnp.bfloat16)
    attended = (
        jnp.einsum(
            "ihst,ithd->ishd", weights_soft, qkv_heads[2], preferred_element_type=jnp.float32
        )
        .astype(jnp.bfloat16)
        .reshape(images, length, -1)
    )
    middle = start_rows + sum_rows(
        jnp.einsum("ish,hd->isd", attended, w_attn, preferred_element_type=jnp.float32)
    )
    normed_two, unit_two, factor_two = normalize(middle, gain_rows[1], shift_rows[1])
    own_two = normed_two.astype(jnp.bfloat16)
    full_two = gather_rows(own_two)
    logits = jnp.einsum("isd,de->ise", full_two, w_router, preferred_element_type=jnp.float32)
    pick_table = (expert_picks[..., None] == jnp.arange(experts)).astype(jnp.float32)
    chosen = jnp.sum(pick_table * logits[:, :, None, :], axis=-1)
    first_gate = jax.nn.sigmoid(chosen[..., 0] - chosen[..., 1])
    gate_pair = jnp.stack([first_gate, 1.0 - first_gate], axis=-1)
    cell_index = jnp.where(slot_picks < capacity, expert_picks * capacity + slot_picks, dump_cell)
    copies = jnp.broadcast_to(full_two[:, :, None, :], (images, length, 2, feature_count)).reshape(
        -1, feature_count
    )
    sending = (
        jnp.zeros((dump_cell + 1, feature_count), jnp.bfloat16)
        .at[cell_index.reshape(-1)]
        .set(copies)
    )
    sending = sending[:dump_cell].reshape(owner_count, local_count, capacity, feature_count)
    arrived = lax.all_to_all(sending, "expert", split_axis=0, concat_axis=0, tiled=True)
    inner_rows = jnp.einsum("sjcd,jdf->sjcf", arrived, w_first, preferred_element_type=jnp.float32)
    hidden = gelu_value(inner_rows).astype(jnp.bfloat16)
    partial_out = jnp.einsum("sjcf,jfd->sjcd", hidden, w_second, preferred_element_type=jnp.float32)
    zero_row = jnp.zeros((1, feature_count), jnp.float32)
    returned = lax.all_to_all(
        partial_out.astype(jnp.bfloat16), "expert", split_axis=0, concat_axis=0, tiled=True
    ).astype(partial_out.dtype)
    table_out = jnp.concatenate([returned.reshape(dump_cell, feature_count), zero_row], axis=0)
    mixed_rows = sum_rows(jnp.sum(gate_pair[..., None] * table_out[cell_index], axis=2))
    result = (middle + mixed_rows).astype(jnp.bfloat16)
    kept_state = (
        unit_one,
        factor_one,
        full_one,
        qkv_rows,
        log_total,
        attended,
        unit_two,
        factor_two,
        own_two,
        full_two,
        pick_table,
        gate_pair,
        cell_index,
        arrived,
        inner_rows,
        hidden,
        table_out,
    )
    return (result, kept_state)


def backward(grad_rows, weights_all, expert_picks, kept_state):
    gain_rows, shift_rows, w_qkv, w_attn, w_router, w_first, w_second = weights_all
    (
        unit_one,
        factor_one,
        full_one,
        qkv_rows,
        log_total,
        attended,
        unit_two,
        factor_two,
        own_two,
        full_two,
        pick_table,
        gate_pair,
        cell_index,
        arrived,
        inner_rows,
        hidden,
        table_out,
    ) = kept_state
    images = expert_picks.shape[0]
    length = expert_picks.shape[1]
    feature_count = grad_rows.shape[2]
    experts = w_router.shape[1]
    capacity = 2 * images * length // experts
    dump_cell = experts * capacity
    owner_count = lax.axis_size("expert")
    local_count = experts // owner_count
    score_scale = HEAD_DIM ** (-0.5)
    head_count = w_qkv.shape[2] // HEAD_DIM
    full_grad = gather_rows(grad_rows.astype(jnp.bfloat16))
    full_wide = full_grad.astype(jnp.float32)
    pieces = (
        (gate_pair[..., None] * full_wide[:, :, None, :])
        .astype(jnp.bfloat16)
        .reshape(-1, feature_count)
    )
    back_send = (
        jnp.zeros((dump_cell + 1, feature_count), jnp.bfloat16)
        .at[cell_index.reshape(-1)]
        .set(pieces)
    )
    back_send = back_send[:dump_cell].reshape(owner_count, local_count, capacity, feature_count)
    back_arrived = lax.all_to_all(back_send, "expert", split_axis=0, concat_axis=0, tiled=True)
    hidden_grad = jnp.einsum(
        "sjcd,jfd->sjcf", back_arrived, w_second, preferred_element_type=jnp.float32
    )
    inner_grad = (hidden_grad * gelu_slope(inner_rows)).astype(jnp.bfloat16)
    grad_second = jnp.einsum(
        "sjcf,sjcd->jfd", hidden, back_arrived, preferred_element_type=jnp.float32
    )
    grad_first = jnp.einsum(
        "sjcd,sjcf->jdf", arrived, inner_grad, preferred_element_type=jnp.float32
    )
    input_part = jnp.einsum(
        "sjcf,jdf->sjcd", inner_grad, w_first, preferred_element_type=jnp.float32
    )
    zero_row = jnp.zeros((1, feature_count), jnp.float32)
    sign_table = pick_table[:, :, 0, :] - pick_table[:, :, 1, :]
    input_back = lax.all_to_all(
        input_part.astype(jnp.bfloat16), "expert", split_axis=0, concat_axis=0, tiled=True
    ).astype(input_part.dtype)
    table_in = jnp.concatenate([input_back.reshape(dump_cell, feature_count), zero_row], axis=0)
    routed = jnp.sum(table_in[cell_index], axis=2)
    gate_grad = jnp.sum(full_wide[:, :, None, :] * table_out[cell_index], axis=-1)
    logit_grad = (gate_pair[..., 0] * gate_pair[..., 1] * (gate_grad[..., 0] - gate_grad[..., 1]))[
        ..., None
    ] * sign_table
    grad_router = jnp.einsum(
        "isd,ise->de", full_two, logit_grad, precision=highest, preferred_element_type=jnp.float32
    )
    normed_grad = sum_rows(
        routed
        + jnp.einsum(
            "ise,de->isd",
            logit_grad,
            w_router,
            precision=highest,
            preferred_element_type=jnp.float32,
        )
    )
    mid_grad = grad_rows + norm_back(normed_grad, unit_two, factor_two, gain_rows[1])
    gain_two = jnp.sum(normed_grad * unit_two, axis=(0, 1))
    shift_two = jnp.sum(normed_grad, axis=(0, 1))
    full_mid = gather_rows(mid_grad.astype(jnp.bfloat16))
    grad_attn = jnp.einsum("ish,isd->hd", attended, full_mid, preferred_element_type=jnp.float32)
    attended_grad = (
        jnp.einsum("isd,hd->ish", full_mid, w_attn, preferred_element_type=jnp.float32)
        .astype(jnp.bfloat16)
        .reshape(images, length, head_count, HEAD_DIM)
    )
    qkv_heads = qkv_rows.reshape(3, images, length, head_count, HEAD_DIM)
    scores = (
        jnp.einsum(
            "ishd,ithd->ihst", qkv_heads[0], qkv_heads[1], preferred_element_type=jnp.float32
        )
        * score_scale
    )
    probs_wide = jnp.exp(scores - log_total)
    value_grad = jnp.einsum(
        "ihst,ishd->ithd",
        probs_wide.astype(jnp.bfloat16),
        attended_grad,
        preferred_element_type=jnp.float32,
    ).astype(jnp.bfloat16)
    prob_grad = jnp.einsum(
        "ishd,ithd->ihst", attended_grad, qkv_heads[2], preferred_element_type=jnp.float32
    )
    row_dot = jnp.sum(probs_wide * prob_grad, axis=-1, keepdims=True)
    score_grad = (probs_wide * (prob_grad - row_dot) * score_scale).astype(jnp.bfloat16)
    query_grad = jnp.einsum(
        "ihst,ithd->ishd", score_grad, qkv_heads[1], preferred_element_type=jnp.float32
    ).astype(jnp.bfloat16)
    key_grad = jnp.einsum(
        "ihst,ishd->ithd", score_grad, qkv_heads[0], preferred_element_type=jnp.float32
    ).astype(jnp.bfloat16)
    qkv_grad = jnp.stack([query_grad, key_grad, value_grad]).reshape(3, images, length, -1)
    grad_qkv = jnp.einsum("isd,kish->kdh", full_one, qkv_grad, preferred_element_type=jnp.float32)
    first_grad = sum_rows(
        jnp.einsum("kish,kdh->isd", qkv_grad, w_qkv, preferred_element_type=jnp.float32)
    )
    start_grad = mid_grad + norm_back(first_grad, unit_one, factor_one, gain_rows[0])
    gain_one = jnp.sum(first_grad * unit_one, axis=(0, 1))
    shift_one = jnp.sum(first_grad, axis=(0, 1))
    grad_parts = (
        jnp.stack([gain_one, gain_two]),
        jnp.stack([shift_one, shift_two]),
        grad_qkv,
        grad_attn,
        grad_router,
        grad_first,
        grad_second,
    )
    return (start_grad.astype(jnp.bfloat16), grad_parts)


def per_device(
    tokens,
    cotangent,
    norm_gains,
    norm_shifts,
    w_qkv,
    w_attn_out,
    w_router,
    w_in,
    w_out,
    choices,
    slot_ranks,
):
    section_index = lax.axis_index("section")
    micro_count = tokens.shape[0]
    feature_count = tokens.shape[3]
    weights_all = (
        norm_gains[0],
        norm_shifts[0],
        w_qkv[0].reshape(3, feature_count, -1),
        w_attn_out[0].reshape(-1, feature_count),
        w_router[0],
        w_in[0],
        w_out[0],
    )
    received = jnp.zeros(tokens.shape[1:], jnp.bfloat16)
    produced = []
    kept_list = []
    for moment in range(micro_count + 1):
        if moment < micro_count:
            fresh_rows = tokens[moment]
        else:
            fresh_rows = jnp.zeros(tokens.shape[1:], jnp.bfloat16)
        block_rows = jnp.where(section_index == 0, fresh_rows, received)
        micro_index = jnp.clip(moment - section_index, 0, micro_count - 1)
        expert_picks = lax.dynamic_index_in_dim(choices[0], micro_index, 0, keepdims=False)
        slot_picks = lax.dynamic_index_in_dim(slot_ranks[0], micro_index, 0, keepdims=False)
        result, kept_state = forward(block_rows, weights_all, expert_picks, slot_picks)
        received = shifted(result, "section", 1)
        produced.append(result)
        kept_list.append((kept_state, expert_picks))
    section_out = lax.dynamic_slice_in_dim(jnp.stack(produced), section_index, micro_count, 0)[None]
    returned_grad = jnp.zeros(cotangent.shape[1:], jnp.float32)
    input_grads = []
    totals = None
    for moment in range(micro_count + 1):
        micro_late = micro_count - 1 - moment
        if micro_late >= 0:
            outer_grad = cotangent[micro_late]
        else:
            outer_grad = jnp.zeros(cotangent.shape[1:], jnp.float32)
        grad_rows = jnp.where(section_index == 1, outer_grad, returned_grad)
        kept_state, expert_picks = kept_list[micro_count - moment]
        grad_input, grad_parts = backward(grad_rows, weights_all, expert_picks, kept_state)
        returned_grad = shifted(grad_input, "section", -1).astype(jnp.float32)
        input_grads.append(grad_input)
        totals = grad_parts if totals is None else jax.tree.map(jnp.add, totals, grad_parts)
    input_grad = lax.dynamic_slice_in_dim(
        jnp.stack(input_grads[::-1]), section_index, micro_count, 0
    )[None]
    gain_sum, shift_sum, qkv_sum, attn_sum, router_sum, first_sum, second_sum = totals
    qkv_total, attn_total = (
        lax.psum(qkv_sum.astype(jnp.bfloat16), "expert").astype(jnp.float32),
        lax.psum(attn_sum.astype(jnp.bfloat16), "expert").astype(jnp.float32),
    )
    gain_total, shift_total, router_total = lax.psum(
        (gain_sum, shift_sum, router_sum), ("tensor", "expert")
    )
    return (
        section_out,
        input_grad,
        gain_total[None],
        shift_total[None],
        qkv_total.reshape(w_qkv.shape),
        attn_total.reshape(w_attn_out.shape),
        router_total[None],
        first_sum[None],
        second_sum[None],
    )


def solution(mesh):
    return jax.shard_map(
        per_device,
        mesh=mesh,
        in_specs=(
            P(None, "expert", "tensor", None),
            P(None, "expert", "tensor", None),
            P("section", None, None),
            P("section", None, None),
            P("section", None, None, "tensor", None),
            P("section", "tensor", None, None),
            P("section", None, None),
            P("section", "expert", None, "tensor"),
            P("section", "expert", "tensor", None),
            P("section", None, "expert", None, None),
            P("section", None, "expert", None, None),
        ),
        out_specs=(
            P("section", None, "expert", "tensor", None),
            P("section", None, "expert", "tensor", None),
            P("section", None, None),
            P("section", None, None),
            P("section", None, None, "tensor", None),
            P("section", "tensor", None, None),
            P("section", None, None),
            P("section", "expert", None, "tensor"),
            P("section", "expert", "tensor", None),
        ),
        check_vma=False,
    )
```

profile of v0, /device:TPU:0, one launch (start us, length us, event | category | flops | bytes accessed | tf_op | source)
XLA Modules:
  0.0 1035.5 jit_solution(583829729808899617)
XLA Ops:
  11.4 11.0 %all_gather.36 = bf16[1,256,768]{2,1,0:T(8,128)(2,1)S(1)} all-gather(bf16[1,64,768]{2,1,0:T(8,128)(2,1)S(1)} %fusion.265), channel_id=1, replica_groups=mesh['section'=2,'tensor'=4,'expert'=4] {'tensor'}, dimensions={1}, use_global_device_ids=true | all-gather | bytes 491520 | tf_op jit(solution)/shard_map/all_gather | solution.py:48
  29.3 24.2 %reduce-scatter.13.cloned.1.call-done = bf16[1,64,768]{2,1,0:T(8,128)(2,1)} async-done(((bf16[1,256,768]{2,1,0:T(8,128)(2,1)}), bf16[1,64,768]{2,1,0:T(8,128)(2,1)}) %reduce-scatter.13.cloned.1.call-update) | async-done | bytes 98320 | tf_op jit(solution)/shard_map/reduce_scatter | solution.py:52
  76.3 21.7 %all_to_all.60 = bf16[4,2,64,768]{3,2,1,0:T(8,128)(2,1)S(1)} all-to-all(bf16[4,2,64,768]{3,2,1,0:T(8,128)(2,1)S(1)} %bitcast.669), channel_id=1, replica_groups=mesh['section'=2,'tensor'=4,'expert'=4] {'expert'}, dimensions={0} | all-to-all | bytes 1572864 | tf_op jit(solution)/shard_map/all_to_all | solution.py:112
  107.6 16.3 %all-to-all-done.1 = bf16[4,2,64,768]{3,2,1,0:T(8,128)(2,1)} async-done(((bf16[4,2,64,768]{3,2,1,0:T(8,128)(2,1)}), bf16[4,2,64,768]{3,2,1,0:T(8,128)(2,1)}, u32[]{:S(2)}, u32[]{:S(2)}) %all-to-all-start.1) | async-done | bytes 786464 | tf_op jit(solution)/shard_map/all_to_all | solution.py:117
  138.1 22.9 %reduce-scatter.15.cloned.1.call-done = bf16[1,64,768]{2,1,0:T(8,128)(2,1)} async-done(((bf16[1,256,768]{2,1,0:T(8,128)(2,1)}), bf16[1,64,768]{2,1,0:T(8,128)(2,1)}) %reduce-scatter.15.cloned.1.call-update) | async-done | bytes 98320 | tf_op jit(solution)/shard_map/reduce_scatter | solution.py:52
  184.1 22.5 %reduce-scatter.17.cloned.1.call-done = bf16[1,64,768]{2,1,0:T(8,128)(2,1)} async-done(((bf16[1,256,768]{2,1,0:T(8,128)(2,1)}), bf16[1,64,768]{2,1,0:T(8,128)(2,1)}) %reduce-scatter.17.cloned.1.call-update) | async-done | bytes 98320 | tf_op jit(solution)/shard_map/reduce_scatter | solution.py:52
  229.4 22.2 %all_to_all.61 = bf16[4,2,64,768]{3,2,1,0:T(8,128)(2,1)S(1)} all-to-all(bf16[4,2,64,768]{3,2,1,0:T(8,128)(2,1)S(1)} %bitcast.670), channel_id=1, replica_groups=mesh['section'=2,'tensor'=4,'expert'=4] {'expert'}, dimensions={0} | all-to-all | bytes 1572864 | tf_op jit(solution)/shard_map/all_to_all | solution.py:112
  260.2 17.1 %all-to-all-done.3 = bf16[4,2,64,768]{3,2,1,0:T(8,128)(2,1)} async-done(((bf16[4,2,64,768]{3,2,1,0:T(8,128)(2,1)}), bf16[4,2,64,768]{3,2,1,0:T(8,128)(2,1)}, u32[]{:S(2)}, u32[]{:S(2)}) %all-to-all-start.3) | async-done | bytes 786464 | tf_op jit(solution)/shard_map/all_to_all | solution.py:117
  291.6 22.9 %reduce-scatter.19.cloned.1.call-done = bf16[1,64,768]{2,1,0:T(8,128)(2,1)} async-done(((bf16[1,256,768]{2,1,0:T(8,128)(2,1)}), bf16[1,64,768]{2,1,0:T(8,128)(2,1)}) %reduce-scatter.19.cloned.1.call-update) | async-done | bytes 98320 | tf_op jit(solution)/shard_map/reduce_scatter | solution.py:52
  332.9 24.6 %reduce-scatter.21.cloned.1.call-done = bf16[1,64,768]{2,1,0:T(8,128)(2,1)} async-done(((bf16[1,256,768]{2,1,0:T(8,128)(2,1)}), bf16[1,64,768]{2,1,0:T(8,128)(2,1)}) %reduce-scatter.21.cloned.1.call-update) | async-done | bytes 98320 | tf_op jit(solution)/shard_map/reduce_scatter | solution.py:52
  360.7 10.1 all_gather.41
  416.9 12.5 %all-to-all-done.6 = bf16[4,2,64,768]{3,2,1,0:T(8,128)(2,1)} async-done(((bf16[4,2,64,768]{3,2,1,0:T(8,128)(2,1)}), bf16[4,2,64,768]{3,2,1,0:T(8,128)(2,1)}, u32[]{:S(2)}, u32[]{:S(2)}) %all-to-all-start.6) | async-done | bytes 786464 | tf_op jit(solution)/shard_map/all_to_all | solution.py:189
  441.6 13.4 %all-to-all-done.7 = bf16[4,2,64,768]{3,2,1,0:T(8,128)(2,1)} async-done(((bf16[4,2,64,768]{3,2,1,0:T(8,128)(2,1)}), bf16[4,2,64,768]{3,2,1,0:T(8,128)(2,1)}, u32[]{:S(2)}, u32[]{:S(2)}) %all-to-all-start.7) | async-done | bytes 786464 | tf_op jit(solution)/shard_map/all_to_all | solution.py:205
  501.8 20.1 %reduce-scatter.25.cloned.1.call-done = bf16[1,64,768]{2,1,0:T(8,128)(2,1)} async-done(((bf16[1,256,768]{2,1,0:T(8,128)(2,1)}), bf16[1,64,768]{2,1,0:T(8,128)(2,1)}) %reduce-scatter.25.cloned.1.call-update) | async-done | bytes 98320 | tf_op jit(solution)/shard_map/reduce_scatter | solution.py:52
  524.0 26.0 %reduce-scatter.23.cloned.1.call-done = bf16[1,64,768]{2,1,0:T(8,128)(2,1)} async-done(((bf16[1,256,768]{2,1,0:T(8,128)(2,1)}), bf16[1,64,768]{2,1,0:T(8,128)(2,1)}) %reduce-scatter.23.cloned.1.call-update) | async-done | bytes 98320 | tf_op jit(solution)/shard_map/reduce_scatter | solution.py:52
  551.6 10.3 all_gather.43
  576.6 24.9 %reduce-scatter.27.cloned.1.call-done = bf16[1,64,768]{2,1,0:T(8,128)(2,1)} async-done(((bf16[1,256,768]{2,1,0:T(8,128)(2,1)}), bf16[1,64,768]{2,1,0:T(8,128)(2,1)}) %reduce-scatter.27.cloned.1.call-update) | async-done | bytes 98320 | tf_op jit(solution)/shard_map/reduce_scatter | solution.py:52
  628.7 22.8 %all_to_all.62 = bf16[4,2,64,768]{3,2,1,0:T(8,128)(2,1)S(1)} all-to-all(bf16[4,2,64,768]{3,2,1,0:T(8,128)(2,1)S(1)} %bitcast.665), channel_id=1, replica_groups=mesh['section'=2,'tensor'=4,'expert'=4] {'expert'}, dimensions={0} | all-to-all | bytes 1572864 | tf_op jit(solution)/shard_map/all_to_all | solution.py:189
  665.6 12.9 %all-to-all-done.9 = bf16[4,2,64,768]{3,2,1,0:T(8,128)(2,1)} async-done(((bf16[4,2,64,768]{3,2,1,0:T(8,128)(2,1)}), bf16[4,2,64,768]{3,2,1,0:T(8,128)(2,1)}, u32[]{:S(2)}, u32[]{:S(2)}) %all-to-all-start.9) | async-done | bytes 786464 | tf_op jit(solution)/shard_map/all_to_all | solution.py:205
  698.0 20.4 %reduce-scatter.29.cloned.1.call-done = bf16[1,64,768]{2,1,0:T(8,128)(2,1)} async-done(((bf16[1,256,768]{2,1,0:T(8,128)(2,1)}), bf16[1,64,768]{2,1,0:T(8,128)(2,1)}) %reduce-scatter.29.cloned.1.call-update) | async-done | bytes 98320 | tf_op jit(solution)/shard_map/reduce_scatter | solution.py:52
  745.8 23.7 %reduce-scatter.31.cloned.1.call-done = bf16[1,64,768]{2,1,0:T(8,128)(2,1)} async-done(((bf16[1,256,768]{2,1,0:T(8,128)(2,1)}), bf16[1,64,768]{2,1,0:T(8,128)(2,1)}) %reduce-scatter.31.cloned.1.call-update) | async-done | bytes 98320 | tf_op jit(solution)/shard_map/reduce_scatter | solution.py:52
  775.9 10.5 %all_gather.46 = bf16[1,256,768]{2,1,0:T(8,128)(2,1)S(1)} all-gather(bf16[1,64,768]{2,1,0:T(8,128)(2,1)S(1)} %fusion.298), channel_id=1, replica_groups=mesh['section'=2,'tensor'=4,'expert'=4] {'tensor'}, dimensions={1}, use_global_device_ids=true | all-gather | bytes 491520 | tf_op jit(solution)/shard_map/all_gather | solution.py:48
  877.0 12.3 %reduce-scatter.33.cloned.1.call-done = bf16[1,64,768]{2,1,0:T(8,128)(2,1)} async-done(((bf16[1,256,768]{2,1,0:T(8,128)(2,1)}), bf16[1,64,768]{2,1,0:T(8,128)(2,1)}) %reduce-scatter.33.cloned.1.call-update) | async-done | bytes 98320 | tf_op jit(solution)/shard_map/reduce_scatter | solution.py:52
  942.5 79.7 %all-reduce.6 = (f32[1,2,768]{2,1,0:T(2,128)}, f32[1,2,768]{2,1,0:T(2,128)}, f32[1,768,8]{1,2,0:T(8,128)}) all-reduce(f32[1,2,768]{2,1,0:T(2,128)S(1)} %fusion.357, f32[1,2,768]{2,1,0:T(2,128)S(1)} %fusion.359, f32[1,768,8]{1,2,0:T(8,128)} %fusion.144), channel_id=1, replica_groups=mesh['section'=2,'tensor'=4,'expert'=4] {'tensor','expert'}, use_global_device_ids=true, to_apply=%region_66.67 | all-reduce | flops 9216 | bytes 73728 | tf_op jit(solution)/shard_map/psum | solution.py:347
  (618 shorter events, 514.2 us)
Async XLA Ops:
  7.2 46.3 %reduce-scatter.13.cloned.1.call-start = ((), (), s32[]{:S(2)}) async-start(), calls=%async_computation.24 | async-start | bytes 491520 | tf_op jit(solution)/shard_map/reduce_scatter | solution.py:52
  101.1 22.7 %all-to-all-start.1 = ((bf16[4,2,64,768]{3,2,1,0:T(8,128)(2,1)}), bf16[4,2,64,768]{3,2,1,0:T(8,128)(2,1)}, u32[]{:S(2)}, u32[]{:S(2)}) async-start(bf16[4,2,64,768]{3,2,1,0:T(8,128)(2,1)} %copy.213), calls=%async_computation.2 | async-start | bytes 1572864 | tf_op jit(solution)/shard_map/all_to_all | solution.py:117
  105.3 55.7 %reduce-scatter.15.cloned.1.call-start = ((), (), s32[]{:S(2)}) async-start(), calls=%async_computation.25 | async-start | bytes 491520 | tf_op jit(solution)/shard_map/reduce_scatter | solution.py:52
  138.0 68.6 %reduce-scatter.17.cloned.1.call-start = ((), (), s32[]{:S(2)}) async-start(), calls=%async_computation.26 | async-start | bytes 491520 | tf_op jit(solution)/shard_map/reduce_scatter | solution.py:52
  254.6 22.7 %all-to-all-start.3 = ((bf16[4,2,64,768]{3,2,1,0:T(8,128)(2,1)}), bf16[4,2,64,768]{3,2,1,0:T(8,128)(2,1)}, u32[]{:S(2)}, u32[]{:S(2)}) async-start(bf16[4,2,64,768]{3,2,1,0:T(8,128)(2,1)} %copy.219), calls=%async_computation.6 | async-start | bytes 1572864 | tf_op jit(solution)/shard_map/all_to_all | solution.py:117
  258.8 55.7 %reduce-scatter.19.cloned.1.call-start = ((), (), s32[]{:S(2)}) async-start(), calls=%async_computation.27 | async-start | bytes 491520 | tf_op jit(solution)/shard_map/reduce_scatter | solution.py:52
  291.5 66.0 %reduce-scatter.21.cloned.1.call-start = ((), (), s32[]{:S(2)}) async-start(), calls=%async_computation.28 | async-start | bytes 491520 | tf_op jit(solution)/shard_map/reduce_scatter | solution.py:52
  381.2 26.7 %all-to-all-start.4 = ((bf16[4,2,64,768]{3,2,1,0:T(8,128)(2,1)}), bf16[4,2,64,768]{3,2,1,0:T(8,128)(2,1)}, u32[]{:S(2)}, u32[]{:S(2)}) async-start(bf16[4,2,64,768]{3,2,1,0:T(8,128)(2,1)} %bitcast.666), calls=%async_computation.9 | async-start | bytes 1572864 | tf_op jit(solution)/shard_map/all_to_all | solution.py:112
  408.0 21.4 %all-to-all-start.6 = ((bf16[4,2,64,768]{3,2,1,0:T(8,128)(2,1)}), bf16[4,2,64,768]{3,2,1,0:T(8,128)(2,1)}, u32[]{:S(2)}, u32[]{:S(2)}) async-start(bf16[4,2,64,768]{3,2,1,0:T(8,128)(2,1)} %bitcast.668), calls=%async_computation.12 | async-start | bytes 1572864 | tf_op jit(solution)/shard_map/all_to_all | solution.py:189
  434.0 21.0 %all-to-all-start.7 = ((bf16[4,2,64,768]{3,2,1,0:T(8,128)(2,1)}), bf16[4,2,64,768]{3,2,1,0:T(8,128)(2,1)}, u32[]{:S(2)}, u32[]{:S(2)}) async-start(bf16[4,2,64,768]{3,2,1,0:T(8,128)(2,1)} %copy.229), calls=%async_computation.13 | async-start | bytes 1572864 | tf_op jit(solution)/shard_map/all_to_all | solution.py:205
  455.0 21.7 %all-to-all-start.5 = ((bf16[4,2,64,768]{3,2,1,0:T(8,128)(2,1)}), bf16[4,2,64,768]{3,2,1,0:T(8,128)(2,1)}, u32[]{:S(2)}, u32[]{:S(2)}) async-start(bf16[4,2,64,768]{3,2,1,0:T(8,128)(2,1)} %copy.225), calls=%async_computation.10 | async-start | bytes 1572864 | tf_op jit(solution)/shard_map/all_to_all | solution.py:117
  459.2 62.6 %reduce-scatter.25.cloned.1.call-start = ((), (), s32[]{:S(2)}) async-start(), calls=%async_computation.30 | async-start | bytes 491520 | tf_op jit(solution)/shard_map/reduce_scatter | solution.py:52
  498.5 51.5 %reduce-scatter.23.cloned.1.call-start = ((), (), s32[]{:S(2)}) async-start(), calls=%async_computation.29 | async-start | bytes 491520 | tf_op jit(solution)/shard_map/reduce_scatter | solution.py:52
  499.2 102.2 %reduce-scatter.27.cloned.1.call-start = ((), (), s32[]{:S(2)}) async-start(), calls=%async_computation.31 | async-start | bytes 491520 | tf_op jit(solution)/shard_map/reduce_scatter | solution.py:52
  604.7 3.4 collective-permute-start.2
  655.3 23.3 %all-to-all-start.9 = ((bf16[4,2,64,768]{3,2,1,0:T(8,128)(2,1)}), bf16[4,2,64,768]{3,2,1,0:T(8,128)(2,1)}, u32[]{:S(2)}, u32[]{:S(2)}) async-start(bf16[4,2,64,768]{3,2,1,0:T(8,128)(2,1)} %copy.239), calls=%async_computation.17 | async-start | bytes 1572864 | tf_op jit(solution)/shard_map/all_to_all | solution.py:205
  659.5 58.9 %reduce-scatter.29.cloned.1.call-start = ((), (), s32[]{:S(2)}) async-start(), calls=%async_computation.32 | async-start | bytes 491520 | tf_op jit(solution)/shard_map/reduce_scatter | solution.py:52
  695.4 74.2 %reduce-scatter.31.cloned.1.call-start = ((), (), s32[]{:S(2)}) async-start(), calls=%async_computation.33 | async-start | bytes 491520 | tf_op jit(solution)/shard_map/reduce_scatter | solution.py:52
  772.3 3.5 collective-permute-start.3
  797.8 24.5 %all-to-all-start.10 = ((bf16[4,2,64,768]{3,2,1,0:T(8,128)(2,1)}), bf16[4,2,64,768]{3,2,1,0:T(8,128)(2,1)}, u32[]{:S(2)}, u32[]{:S(2)}) async-start(bf16[4,2,64,768]{3,2,1,0:T(8,128)(2,1)} %bitcast.667), calls=%async_computation.20 | async-start | bytes 1572864 | tf_op jit(solution)/shard_map/all_to_all | solution.py:189
  827.0 23.9 %all-to-all-start.11 = ((bf16[4,2,64,768]{3,2,1,0:T(8,128)(2,1)}), bf16[4,2,64,768]{3,2,1,0:T(8,128)(2,1)}, u32[]{:S(2)}, u32[]{:S(2)}) async-start(bf16[4,2,64,768]{3,2,1,0:T(8,128)(2,1)} %copy.249), calls=%async_computation.21 | async-start | bytes 1572864 | tf_op jit(solution)/shard_map/all_to_all | solution.py:205
  831.2 58.1 %reduce-scatter.33.cloned.1.call-start = ((), (), s32[]{:S(2)}) async-start(), calls=%async_computation.34 | async-start | bytes 491520 | tf_op jit(solution)/shard_map/reduce_scatter | solution.py:52
  866.4 73.5 %reduce-scatter.35.cloned.1.call-start = ((), (), s32[]{:S(2)}) async-start(), calls=%async_computation.35 | async-start | bytes 491520 | tf_op jit(solution)/shard_map/reduce_scatter | solution.py:52
  915.0 110.0 %all-reduce.10.cloned.1.call-start = ((), (), s32[]{:S(2)}) async-start(), calls=%async_computation.36 | async-start | bytes 2359296 | tf_op jit(solution)/shard_map/psum | solution.py:344
  (155 other events, 2669.0 us)
Sparse Core Ops, SparseCore 0:
  28.5 25.0 reduce-scatter.12
  138.1 22.8 reduce-scatter.14
  181.8 24.7 reduce-scatter.16
  291.7 22.8 reduce-scatter.18
  332.7 24.7 reduce-scatter.20
  498.6 23.2 reduce-scatter.24
  525.2 24.6 reduce-scatter.22
  576.7 24.7 reduce-scatter.26
  695.5 22.8 reduce-scatter.28
  744.8 24.7 reduce-scatter.30
  866.4 22.8 reduce-scatter.32
  915.1 24.7 reduce-scatter.34
  942.9 57.7 all-reduce.9
where the time goes:
time: 1050 us; the launch traced here: 1040 us
  waiting for transfers between devices  348 us (33%)
  blocking collectives  264 us (25%)
  local copies, waits for them, and re-layouts  125 us (12%)
  matrix products  124 us (12%)
  other arithmetic  112 us (11%)
  starting transfers between devices  46.3 us (4%)
  between operations  16.3 us (2%)
    reduce_scatter x12, waiting for transfers between devices, sum_rows(): lax.psum_scatter(block_terms.astype(jnp.bfloat16), 'tensor', scatter_dime...  251 us
    all_gather x12, blocking collectives, gather_rows(): return lax.all_gather(block_part, 'tensor', axis=1, tiled=True)  118 us
    psum x1, blocking collectives, per_device(): lax.psum((gain_sum, shift_sum, router_sum), ('tensor', 'expert'))  79.7 us
    all_to_all x2, blocking collectives, forward(): lax.all_to_all(sending, 'expert', split_axis=0, concat_axis=0, tiled=True)  43.9 us
    all_to_all x3, waiting for transfers between devices, forward(): lax.all_to_all(partial_out.astype(jnp.bfloat16), 'expert', split_axis=0,...  40.3 us
    all_to_all x3, waiting for transfers between devices, backward(): lax.all_to_all(input_part.astype(jnp.bfloat16), 'expert', split_axis=0, c...  33.5 us
    gather x6, local copies, waits for them, and re-layouts, backward(): routed = jnp.sum(table_in[cell_index], axis=2)  22.9 us
    gather x6, local copies, waits for them, and re-layouts, forward(): table_out[cell_index]  22.9 us
  transfers between devices with their start and end apart: 26, of which 23 were waited for; matrix products, arithmetic and copies ran while one was open for 11% of the time, Pallas kernels for 0%

commit v1 on v0

--- a/solution.py
+++ b/solution.py
@@ -345,7 +345,7 @@
         lax.psum(attn_sum.astype(jnp.bfloat16), "expert").astype(jnp.float32),
     )
     gain_total, shift_total, router_total = lax.psum(
-        (gain_sum, shift_sum, router_sum), ("tensor", "expert")
+        lax.psum((gain_sum, shift_sum, router_sum), "expert"), "tensor"
     )
     return (
         section_out,

time: 1050 us -> 1020 us (0.971)
  blocking collectives: 264 us -> 223 us
  waiting for transfers between devices: 348 us -> 364 us
    psum x1 -> x2, blocking collectives: 79.7 us -> 38 us  [the longest x1 21.6 us: per_device(): lax.psum((gain_sum, shift_sum, router_sum), 'expert')]
    psum x1, waiting for transfers between devices: 0.01 us -> 16.5 us  [per_device(): lax.psum(qkv_sum.astype(jnp.bfloat16), 'expert').astype(jnp.float32)]
  transfers between devices with their start and end apart: 26 -> 26, of which waited for: 23 -> 24; matrix products, arithmetic and copies ran while one was open for 11% -> 11% of each run, Pallas kernels for 0% -> 0%
where the time goes in v1:
time: 1020 us; the launch traced here: 1010 us
  waiting for transfers between devices  364 us (36%)
  blocking collectives  223 us (22%)
  local copies, waits for them, and re-layouts  125 us (12%)
  matrix products  124 us (12%)
  other arithmetic  112 us (11%)
  starting transfers between devices  46.3 us (5%)
  between operations  16.3 us (2%)
    reduce_scatter x12, waiting for transfers between devices, sum_rows(): lax.psum_scatter(block_terms.astype(jnp.bfloat16), 'tensor', scatter_dime...  251 us
    all_gather x12, blocking collectives, gather_rows(): return lax.all_gather(block_part, 'tensor', axis=1, tiled=True)  118 us
    all_to_all x2, blocking collectives, forward(): lax.all_to_all(sending, 'expert', split_axis=0, concat_axis=0, tiled=True)  43.9 us
    all_to_all x3, waiting for transfers between devices, forward(): lax.all_to_all(partial_out.astype(jnp.bfloat16), 'expert', split_axis=0,...  40.3 us
    all_to_all x3, waiting for transfers between devices, backward(): lax.all_to_all(input_part.astype(jnp.bfloat16), 'expert', split_axis=0, c...  33.5 us
    gather x6, local copies, waits for them, and re-layouts, backward(): routed = jnp.sum(table_in[cell_index], axis=2)  22.9 us
    gather x6, local copies, waits for them, and re-layouts, forward(): table_out[cell_index]  22.9 us
    all_to_all x1, blocking collectives, backward(): lax.all_to_all(back_send, 'expert', split_axis=0, concat_axis=0, tiled=True)  22.8 us
  transfers between devices with their start and end apart: 26, of which 24 were waited for; matrix products, arithmetic and copies ran while one was open for 11% of the time, Pallas kernels for 0%

profile of v1, /device:TPU:0, one launch (start us, length us, event | category | flops | bytes accessed | tf_op | source)
XLA Modules:
  0.0 1010.4 jit_solution(9070218246268693195)
XLA Ops:
  11.4 11.0 %all_gather.36 = bf16[1,256,768]{2,1,0:T(8,128)(2,1)S(1)} all-gather(bf16[1,64,768]{2,1,0:T(8,128)(2,1)S(1)} %fusion.264), channel_id=1, replica_groups=mesh['section'=2,'tensor'=4,'expert'=4] {'tensor'}, dimensions={1}, use_global_device_ids=true | all-gather | bytes 491520 | tf_op jit(solution)/shard_map/all_gather | solution.py:48
  29.3 24.2 %reduce-scatter.13.cloned.1.call-done = bf16[1,64,768]{2,1,0:T(8,128)(2,1)} async-done(((bf16[1,256,768]{2,1,0:T(8,128)(2,1)}), bf16[1,64,768]{2,1,0:T(8,128)(2,1)}) %reduce-scatter.13.cloned.1.call-update) | async-done | bytes 98320 | tf_op jit(solution)/shard_map/reduce_scatter | solution.py:52
  76.3 21.7 %all_to_all.60 = bf16[4,2,64,768]{3,2,1,0:T(8,128)(2,1)S(1)} all-to-all(bf16[4,2,64,768]{3,2,1,0:T(8,128)(2,1)S(1)} %bitcast.666), channel_id=1, replica_groups=mesh['section'=2,'tensor'=4,'expert'=4] {'expert'}, dimensions={0} | all-to-all | bytes 1572864 | tf_op jit(solution)/shard_map/all_to_all | solution.py:112
  107.6 16.3 %all-to-all-done.1 = bf16[4,2,64,768]{3,2,1,0:T(8,128)(2,1)} async-done(((bf16[4,2,64,768]{3,2,1,0:T(8,128)(2,1)}), bf16[4,2,64,768]{3,2,1,0:T(8,128)(2,1)}, u32[]{:S(2)}, u32[]{:S(2)}) %all-to-all-start.1) | async-done | bytes 786464 | tf_op jit(solution)/shard_map/all_to_all | solution.py:117
  138.1 22.9 %reduce-scatter.15.cloned.1.call-done = bf16[1,64,768]{2,1,0:T(8,128)(2,1)} async-done(((bf16[1,256,768]{2,1,0:T(8,128)(2,1)}), bf16[1,64,768]{2,1,0:T(8,128)(2,1)}) %reduce-scatter.15.cloned.1.call-update) | async-done | bytes 98320 | tf_op jit(solution)/shard_map/reduce_scatter | solution.py:52
  184.1 22.5 %reduce-scatter.17.cloned.1.call-done = bf16[1,64,768]{2,1,0:T(8,128)(2,1)} async-done(((bf16[1,256,768]{2,1,0:T(8,128)(2,1)}), bf16[1,64,768]{2,1,0:T(8,128)(2,1)}) %reduce-scatter.17.cloned.1.call-update) | async-done | bytes 98320 | tf_op jit(solution)/shard_map/reduce_scatter | solution.py:52
  229.4 22.2 %all_to_all.61 = bf16[4,2,64,768]{3,2,1,0:T(8,128)(2,1)S(1)} all-to-all(bf16[4,2,64,768]{3,2,1,0:T(8,128)(2,1)S(1)} %bitcast.667), channel_id=1, replica_groups=mesh['section'=2,'tensor'=4,'expert'=4] {'expert'}, dimensions={0} | all-to-all | bytes 1572864 | tf_op jit(solution)/shard_map/all_to_all | solution.py:112
  260.2 17.1 %all-to-all-done.3 = bf16[4,2,64,768]{3,2,1,0:T(8,128)(2,1)} async-done(((bf16[4,2,64,768]{3,2,1,0:T(8,128)(2,1)}), bf16[4,2,64,768]{3,2,1,0:T(8,128)(2,1)}, u32[]{:S(2)}, u32[]{:S(2)}) %all-to-all-start.3) | async-done | bytes 786464 | tf_op jit(solution)/shard_map/all_to_all | solution.py:117
  291.6 22.9 %reduce-scatter.19.cloned.1.call-done = bf16[1,64,768]{2,1,0:T(8,128)(2,1)} async-done(((bf16[1,256,768]{2,1,0:T(8,128)(2,1)}), bf16[1,64,768]{2,1,0:T(8,128)(2,1)}) %reduce-scatter.19.cloned.1.call-update) | async-done | bytes 98320 | tf_op jit(solution)/shard_map/reduce_scatter | solution.py:52
  332.9 24.6 %reduce-scatter.21.cloned.1.call-done = bf16[1,64,768]{2,1,0:T(8,128)(2,1)} async-done(((bf16[1,256,768]{2,1,0:T(8,128)(2,1)}), bf16[1,64,768]{2,1,0:T(8,128)(2,1)}) %reduce-scatter.21.cloned.1.call-update) | async-done | bytes 98320 | tf_op jit(solution)/shard_map/reduce_scatter | solution.py:52
  416.9 12.5 %all-to-all-done.6 = bf16[4,2,64,768]{3,2,1,0:T(8,128)(2,1)} async-done(((bf16[4,2,64,768]{3,2,1,0:T(8,128)(2,1)}), bf16[4,2,64,768]{3,2,1,0:T(8,128)(2,1)}, u32[]{:S(2)}, u32[]{:S(2)}) %all-to-all-start.6) | async-done | bytes 786464 | tf_op jit(solution)/shard_map/all_to_all | solution.py:189
  441.6 13.4 %all-to-all-done.7 = bf16[4,2,64,768]{3,2,1,0:T(8,128)(2,1)} async-done(((bf16[4,2,64,768]{3,2,1,0:T(8,128)(2,1)}), bf16[4,2,64,768]{3,2,1,0:T(8,128)(2,1)}, u32[]{:S(2)}, u32[]{:S(2)}) %all-to-all-start.7) | async-done | bytes 786464 | tf_op jit(solution)/shard_map/all_to_all | solution.py:205
  501.8 20.1 %reduce-scatter.25.cloned.1.call-done = bf16[1,64,768]{2,1,0:T(8,128)(2,1)} async-done(((bf16[1,256,768]{2,1,0:T(8,128)(2,1)}), bf16[1,64,768]{2,1,0:T(8,128)(2,1)}) %reduce-scatter.25.cloned.1.call-update) | async-done | bytes 98320 | tf_op jit(solution)/shard_map/reduce_scatter | solution.py:52
  524.0 26.0 %reduce-scatter.23.cloned.1.call-done = bf16[1,64,768]{2,1,0:T(8,128)(2,1)} async-done(((bf16[1,256,768]{2,1,0:T(8,128)(2,1)}), bf16[1,64,768]{2,1,0:T(8,128)(2,1)}) %reduce-scatter.23.cloned.1.call-update) | async-done | bytes 98320 | tf_op jit(solution)/shard_map/reduce_scatter | solution.py:52
  576.6 24.9 %reduce-scatter.27.cloned.1.call-done = bf16[1,64,768]{2,1,0:T(8,128)(2,1)} async-done(((bf16[1,256,768]{2,1,0:T(8,128)(2,1)}), bf16[1,64,768]{2,1,0:T(8,128)(2,1)}) %reduce-scatter.27.cloned.1.call-update) | async-done | bytes 98320 | tf_op jit(solution)/shard_map/reduce_scatter | solution.py:52
  628.7 22.8 %all_to_all.62 = bf16[4,2,64,768]{3,2,1,0:T(8,128)(2,1)S(1)} all-to-all(bf16[4,2,64,768]{3,2,1,0:T(8,128)(2,1)S(1)} %bitcast.662), channel_id=1, replica_groups=mesh['section'=2,'tensor'=4,'expert'=4] {'expert'}, dimensions={0} | all-to-all | bytes 1572864 | tf_op jit(solution)/shard_map/all_to_all | solution.py:189
  665.6 12.9 %all-to-all-done.9 = bf16[4,2,64,768]{3,2,1,0:T(8,128)(2,1)} async-done(((bf16[4,2,64,768]{3,2,1,0:T(8,128)(2,1)}), bf16[4,2,64,768]{3,2,1,0:T(8,128)(2,1)}, u32[]{:S(2)}, u32[]{:S(2)}) %all-to-all-start.9) | async-done | bytes 786464 | tf_op jit(solution)/shard_map/all_to_all | solution.py:205
  698.0 20.4 %reduce-scatter.29.cloned.1.call-done = bf16[1,64,768]{2,1,0:T(8,128)(2,1)} async-done(((bf16[1,256,768]{2,1,0:T(8,128)(2,1)}), bf16[1,64,768]{2,1,0:T(8,128)(2,1)}) %reduce-scatter.29.cloned.1.call-update) | async-done | bytes 98320 | tf_op jit(solution)/shard_map/reduce_scatter | solution.py:52
  745.8 23.7 %reduce-scatter.31.cloned.1.call-done = bf16[1,64,768]{2,1,0:T(8,128)(2,1)} async-done(((bf16[1,256,768]{2,1,0:T(8,128)(2,1)}), bf16[1,64,768]{2,1,0:T(8,128)(2,1)}) %reduce-scatter.31.cloned.1.call-update) | async-done | bytes 98320 | tf_op jit(solution)/shard_map/reduce_scatter | solution.py:52
  775.9 10.5 %all_gather.46 = bf16[1,256,768]{2,1,0:T(8,128)(2,1)S(1)} all-gather(bf16[1,64,768]{2,1,0:T(8,128)(2,1)S(1)} %fusion.297), channel_id=1, replica_groups=mesh['section'=2,'tensor'=4,'expert'=4] {'tensor'}, dimensions={1}, use_global_device_ids=true | all-gather | bytes 491520 | tf_op jit(solution)/shard_map/all_gather | solution.py:48
  877.0 12.3 %reduce-scatter.33.cloned.1.call-done = bf16[1,64,768]{2,1,0:T(8,128)(2,1)} async-done(((bf16[1,256,768]{2,1,0:T(8,128)(2,1)}), bf16[1,64,768]{2,1,0:T(8,128)(2,1)}) %reduce-scatter.33.cloned.1.call-update) | async-done | bytes 98320 | tf_op jit(solution)/shard_map/reduce_scatter | solution.py:52
  942.5 21.6 %all-reduce.6 = (f32[2,768]{1,0:T(2,128)S(1)}, f32[2,768]{1,0:T(2,128)S(1)}, f32[768,8]{0,1:T(8,128)S(1)}) all-reduce(f32[2,768]{1,0:T(2,128)S(1)} %fusion.355, f32[2,768]{1,0:T(2,128)S(1)} %fusion.356, f32[768,8]{0,1:T(8,128)} %convolution_add_fusion.5), channel_id=1, replica_groups=mesh['section'=2,'tensor'=4,'expert'=4] {'expert'}, use_global_device_ids=true, to_apply=%region_66.67 | all-reduce | flops 9216 | bytes 73728 | tf_op jit(solution)/shard_map/psum | solution.py:348
  964.1 16.4 %all-reduce.7 = (f32[1,2,768]{2,1,0:T(2,128)}, f32[1,2,768]{2,1,0:T(2,128)}, f32[1,768,8]{1,2,0:T(8,128)}) all-reduce(f32[1,2,768]{2,1,0:T(2,128)S(1)} %bitcast.736, f32[1,2,768]{2,1,0:T(2,128)S(1)} %bitcast.737, f32[1,768,8]{1,2,0:T(8,128)S(1)} %bitcast.723), channel_id=1, replica_groups=mesh['section'=2,'tensor'=4,'expert'=4] {'tensor'}, use_global_device_ids=true, to_apply=%region_67.68 | all-reduce | flops 9216 | bytes 73728 | tf_op jit(solution)/shard_map/psum | solution.py:347
  983.4 16.5 %all-reduce.11.cloned.1.call-done = (bf16[1,3,768,3,64]{2,4,3,1,0:T(8,128)(2,1)}, bf16[1,3,64,768]{3,2,1,0:T(8,128)(2,1)}) async-done(((bf16[1,3,768,3,64]{2,4,3,1,0:T(8,128)(2,1)}, bf16[1,3,64,768]{3,2,1,0:T(8,128)(2,1)}), (bf16[1,3,768,3,64]{2,4,3,1,0:T(8,128)(2,1)}, bf16[1,3,64,768]{3,2,1,0:T(8,128)(2,1)})) %all-reduce.11.cloned.1.call-update) | async-done | bytes 1179664 | tf_op jit(solution)/shard_map/psum | solution.py:344
  (619 shorter events, 534.5 us)
Async XLA Ops:
  7.2 46.3 %reduce-scatter.13.cloned.1.call-start = ((), (), s32[]{:S(2)}) async-start(), calls=%async_computation.24 | async-start | bytes 491520 | tf_op jit(solution)/shard_map/reduce_scatter | solution.py:52
  101.1 22.7 %all-to-all-start.1 = ((bf16[4,2,64,768]{3,2,1,0:T(8,128)(2,1)}), bf16[4,2,64,768]{3,2,1,0:T(8,128)(2,1)}, u32[]{:S(2)}, u32[]{:S(2)}) async-start(bf16[4,2,64,768]{3,2,1,0:T(8,128)(2,1)} %copy.213), calls=%async_computation.2 | async-start | bytes 1572864 | tf_op jit(solution)/shard_map/all_to_all | solution.py:117
  105.3 55.7 %reduce-scatter.15.cloned.1.call-start = ((), (), s32[]{:S(2)}) async-start(), calls=%async_computation.25 | async-start | bytes 491520 | tf_op jit(solution)/shard_map/reduce_scatter | solution.py:52
  138.0 68.6 %reduce-scatter.17.cloned.1.call-start = ((), (), s32[]{:S(2)}) async-start(), calls=%async_computation.26 | async-start | bytes 491520 | tf_op jit(solution)/shard_map/reduce_scatter | solution.py:52
  254.6 22.7 %all-to-all-start.3 = ((bf16[4,2,64,768]{3,2,1,0:T(8,128)(2,1)}), bf16[4,2,64,768]{3,2,1,0:T(8,128)(2,1)}, u32[]{:S(2)}, u32[]{:S(2)}) async-start(bf16[4,2,64,768]{3,2,1,0:T(8,128)(2,1)} %copy.219), calls=%async_computation.6 | async-start | bytes 1572864 | tf_op jit(solution)/shard_map/all_to_all | solution.py:117
  258.8 55.7 %reduce-scatter.19.cloned.1.call-start = ((), (), s32[]{:S(2)}) async-start(), calls=%async_computation.27 | async-start | bytes 491520 | tf_op jit(solution)/shard_map/reduce_scatter | solution.py:52
  291.5 66.0 %reduce-scatter.21.cloned.1.call-start = ((), (), s32[]{:S(2)}) async-start(), calls=%async_computation.28 | async-start | bytes 491520 | tf_op jit(solution)/shard_map/reduce_scatter | solution.py:52
  381.2 26.7 %all-to-all-start.4 = ((bf16[4,2,64,768]{3,2,1,0:T(8,128)(2,1)}), bf16[4,2,64,768]{3,2,1,0:T(8,128)(2,1)}, u32[]{:S(2)}, u32[]{:S(2)}) async-start(bf16[4,2,64,768]{3,2,1,0:T(8,128)(2,1)} %bitcast.663), calls=%async_computation.9 | async-start | bytes 1572864 | tf_op jit(solution)/shard_map/all_to_all | solution.py:112
  408.0 21.4 %all-to-all-start.6 = ((bf16[4,2,64,768]{3,2,1,0:T(8,128)(2,1)}), bf16[4,2,64,768]{3,2,1,0:T(8,128)(2,1)}, u32[]{:S(2)}, u32[]{:S(2)}) async-start(bf16[4,2,64,768]{3,2,1,0:T(8,128)(2,1)} %bitcast.665), calls=%async_computation.12 | async-start | bytes 1572864 | tf_op jit(solution)/shard_map/all_to_all | solution.py:189
  434.0 21.0 %all-to-all-start.7 = ((bf16[4,2,64,768]{3,2,1,0:T(8,128)(2,1)}), bf16[4,2,64,768]{3,2,1,0:T(8,128)(2,1)}, u32[]{:S(2)}, u32[]{:S(2)}) async-start(bf16[4,2,64,768]{3,2,1,0:T(8,128)(2,1)} %copy.229), calls=%async_computation.13 | async-start | bytes 1572864 | tf_op jit(solution)/shard_map/all_to_all | solution.py:205
  455.0 21.7 %all-to-all-start.5 = ((bf16[4,2,64,768]{3,2,1,0:T(8,128)(2,1)}), bf16[4,2,64,768]{3,2,1,0:T(8,128)(2,1)}, u32[]{:S(2)}, u32[]{:S(2)}) async-start(bf16[4,2,64,768]{3,2,1,0:T(8,128)(2,1)} %copy.225), calls=%async_computation.10 | async-start | bytes 1572864 | tf_op jit(solution)/shard_map/all_to_all | solution.py:117
  459.2 62.6 %reduce-scatter.25.cloned.1.call-start = ((), (), s32[]{:S(2)}) async-start(), calls=%async_computation.30 | async-start | bytes 491520 | tf_op jit(solution)/shard_map/reduce_scatter | solution.py:52
  498.5 51.5 %reduce-scatter.23.cloned.1.call-start = ((), (), s32[]{:S(2)}) async-start(), calls=%async_computation.29 | async-start | bytes 491520 | tf_op jit(solution)/shard_map/reduce_scatter | solution.py:52
  499.2 102.2 %reduce-scatter.27.cloned.1.call-start = ((), (), s32[]{:S(2)}) async-start(), calls=%async_computation.31 | async-start | bytes 491520 | tf_op jit(solution)/shard_map/reduce_scatter | solution.py:52
  604.7 3.4 collective-permute-start.2
  655.3 23.3 %all-to-all-start.9 = ((bf16[4,2,64,768]{3,2,1,0:T(8,128)(2,1)}), bf16[4,2,64,768]{3,2,1,0:T(8,128)(2,1)}, u32[]{:S(2)}, u32[]{:S(2)}) async-start(bf16[4,2,64,768]{3,2,1,0:T(8,128)(2,1)} %copy.239), calls=%async_computation.17 | async-start | bytes 1572864 | tf_op jit(solution)/shard_map/all_to_all | solution.py:205
  659.5 58.9 %reduce-scatter.29.cloned.1.call-start = ((), (), s32[]{:S(2)}) async-start(), calls=%async_computation.32 | async-start | bytes 491520 | tf_op jit(solution)/shard_map/reduce_scatter | solution.py:52
  695.4 74.2 %reduce-scatter.31.cloned.1.call-start = ((), (), s32[]{:S(2)}) async-start(), calls=%async_computation.33 | async-start | bytes 491520 | tf_op jit(solution)/shard_map/reduce_scatter | solution.py:52
  772.3 3.5 collective-permute-start.3
  797.8 24.5 %all-to-all-start.10 = ((bf16[4,2,64,768]{3,2,1,0:T(8,128)(2,1)}), bf16[4,2,64,768]{3,2,1,0:T(8,128)(2,1)}, u32[]{:S(2)}, u32[]{:S(2)}) async-start(bf16[4,2,64,768]{3,2,1,0:T(8,128)(2,1)} %bitcast.664), calls=%async_computation.20 | async-start | bytes 1572864 | tf_op jit(solution)/shard_map/all_to_all | solution.py:189
  827.0 23.9 %all-to-all-start.11 = ((bf16[4,2,64,768]{3,2,1,0:T(8,128)(2,1)}), bf16[4,2,64,768]{3,2,1,0:T(8,128)(2,1)}, u32[]{:S(2)}, u32[]{:S(2)}) async-start(bf16[4,2,64,768]{3,2,1,0:T(8,128)(2,1)} %copy.249), calls=%async_computation.21 | async-start | bytes 1572864 | tf_op jit(solution)/shard_map/all_to_all | solution.py:205
  831.2 58.1 %reduce-scatter.33.cloned.1.call-start = ((), (), s32[]{:S(2)}) async-start(), calls=%async_computation.34 | async-start | bytes 491520 | tf_op jit(solution)/shard_map/reduce_scatter | solution.py:52
  866.4 73.5 %reduce-scatter.35.cloned.1.call-start = ((), (), s32[]{:S(2)}) async-start(), calls=%async_computation.35 | async-start | bytes 491520 | tf_op jit(solution)/shard_map/reduce_scatter | solution.py:52
  915.0 84.8 %all-reduce.11.cloned.1.call-start = ((), (), s32[]{:S(2)}) async-start(), calls=%async_computation.36 | async-start | bytes 2359296 | tf_op jit(solution)/shard_map/psum | solution.py:344
  (155 other events, 2627.4 us)
Sparse Core Ops, SparseCore 0:
  28.5 25.0 reduce-scatter.12
  138.1 22.8 reduce-scatter.14
  181.8 24.7 reduce-scatter.16
  291.7 22.8 reduce-scatter.18
  332.7 24.7 reduce-scatter.20
  498.6 23.2 reduce-scatter.24
  525.2 24.6 reduce-scatter.22
  576.7 24.7 reduce-scatter.26
  695.5 22.8 reduce-scatter.28
  744.8 24.7 reduce-scatter.30
  866.4 22.8 reduce-scatter.32
  915.1 24.7 reduce-scatter.34
  942.9 56.9 all-reduce.10
